TPU v7x, 32 devices: a whole 2x2x4 slice. The times are simulated.
32 devices in a mesh: grp: 2 (over x), dev: 16 (over z, y, core).
Axes of the slice: x: 2, y: 2, z: 4, core: 2. Of those that a mesh axis runs over, the one named last changes fastest.
Arguments:
- query: bfloat16 [64, 64, 128], P(('grp', 'dev')), may hold values from -6 to 6
- key_cache: bfloat16 [64, 512, 8, 128], P(('grp', 'dev')), may hold values from -6 to 6
- value_cache: bfloat16 [64, 512, 8, 128], P(('grp', 'dev')), may hold values from -6 to 6
- lengths: int32 [64], P(('grp', 'dev')), may hold values from 1 to 512, 16384 in all
- out_weight: bfloat16 [8192, 8192], P('dev', 'grp'), may hold values from -0.0625 to 0.0625
- resid: bfloat16 [64, 8192], P('dev', 'grp'), may hold values from -6 to 6
- norm_gain: bfloat16 [8192], P('grp'), may hold values from 0.5 to 1.5
- gate_weight: bfloat16 [8192, 28672], P('grp', 'dev'), may hold values from -0.0625 to 0.0625
- up_weight: bfloat16 [8192, 28672], P('grp', 'dev'), may hold values from -0.0625 to 0.0625
- down_weight: bfloat16 [28672, 8192], P('dev', 'grp'), may hold values from -0.03125 to 0.03125
Outputs:
- layer_out: bfloat16 [64, 8192], P('dev', 'grp')
Inputs may be any that keep to these rules, and one draw needn't show every extreme that they name: `lengths`: some request has exactly 512 live slots.
All inputs are finite; a program needn't handle non-finite values. No bound on the sum of `lengths` on one device may be relied on, other than what follows from the above.
Results may differ from a plain program's by a relative error of at most 0.015.
Values may be sent and summed in bfloat16 or wider, within the bound.
A program may use at most 128 MiB of HBM per device.

v0:
```python
import jax
import jax.numpy as jnp
from jax import lax
from jax.sharding import PartitionSpec as P


def attend(query, key_cache, value_cache, lengths):
    rows, heads, width = query.shape
    kv_heads = key_cache.shape[2]
    group = heads // kv_heads
    grouped = query.reshape(rows, kv_heads, group, width)
    scores = jnp.einsum(
        "rhgd,rlhd->rhgl", grouped, key_cache, preferred_element_type=jnp.float32
    ) * width ** (-0.5)
    places = jnp.arange(key_cache.shape[1], dtype=jnp.int32)
    valid = places[None, :] < lengths[:, None]
    scores = jnp.where(valid[:, None, None, :], scores, -1e30)
    top = jnp.max(scores, axis=-1, keepdims=True)
    weights = jnp.exp(scores - top)
    probs = (weights / jnp.sum(weights, axis=-1, keepdims=True)).astype(jnp.bfloat16)
    mixed = jnp.einsum("rhgl,rlhd->rhgd", probs, value_cache, preferred_element_type=jnp.float32)
    return mixed.reshape(rows, heads * width).astype(jnp.bfloat16)


def per_device(
    query,
    key_cache,
    value_cache,
    lengths,
    out_weight,
    resid,
    norm_gain,
    gate_weight,
    up_weight,
    down_weight,
):
    attn = attend(query, key_cache, value_cache, lengths)
    block_cols = out_weight.shape[0]
    first_col = lax.axis_index("dev") * block_cols
    cols = lax.dynamic_slice_in_dim(
        lax.all_gather(attn, ("grp", "dev"), axis=0, tiled=True), first_col, block_cols, 1
    )
    proj_terms = jnp.dot(cols, out_weight, preferred_element_type=jnp.float32)
    x = resid.astype(jnp.float32) + lax.psum_scatter(
        proj_terms, "dev", scatter_dimension=0, tiled=True
    )
    width_all = x.shape[1] * lax.axis_size("grp")
    sumsq = lax.psum(jnp.sum(x * x, axis=1), "grp")
    normed = (
        x * lax.rsqrt(sumsq / width_all + 1e-05)[:, None] * norm_gain.astype(jnp.float32)
    ).astype(jnp.bfloat16)
    piece = lax.all_gather(normed, "dev", axis=0, tiled=True)
    half_terms = jnp.concatenate(
        [
            jnp.dot(piece, gate_weight, preferred_element_type=jnp.float32),
            jnp.dot(piece, up_weight, preferred_element_type=jnp.float32),
        ],
        axis=1,
    )
    both = lax.psum(half_terms.astype(jnp.bfloat16), "grp").astype(jnp.float32)
    hidden_cols = gate_weight.shape[1]
    gate = both[:, :hidden_cols]
    up = both[:, hidden_cols:]
    hidden = (jax.nn.silu(gate) * up).astype(jnp.bfloat16)
    ffn_rows = lax.psum_scatter(
        jnp.dot(hidden, down_weight, preferred_element_type=jnp.float32),
        "dev",
        scatter_dimension=0,
        tiled=True,
    )
    return (x + ffn_rows).astype(jnp.bfloat16)


def solution(mesh):
    placed = (
        P(("grp", "dev"), None, None),
        P(("grp", "dev"), None, None, None),
        P(("grp", "dev"), None, None, None),
        P(("grp", "dev")),
        P("dev", "grp"),
        P("dev", "grp"),
        P("grp"),
        P("grp", "dev"),
        P("grp", "dev"),
        P("dev", "grp"),
    )
    return jax.shard_map(
        per_device, mesh=mesh, in_specs=placed, out_specs=P("dev", "grp"), check_vma=False
    )
```

profile of v0, /device:TPU:0, one launch (start us, length us, event | category | flops | bytes accessed | tf_op | source)
XLA Modules:
  0.0 347.9 jit_solution(15746743131024164946)
XLA Ops:
  6.5 0.9 iota_compare_fusion
  7.4 0.7 copy-done
  8.1 1.4 fusion.10
  9.6 0.2 fusion.28
  9.8 2.1 fusion.13
  11.9 0.6 reshape.27
  12.7 56.5 %all-gather.4.cloned.1.call-done = bf16[32,2,8192]{2,1,0:T(2,128)(2,1)} async-done(((bf16[1,2,8192]{2,1,0:T(2,128)(2,1)}), bf16[32,2,8192]{2,1,0:T(2,128)(2,1)}) %all-gather.4.cloned.1.call-update) | async-done | bytes 1048592 | tf_op jit(solution)/shard_map/all_gather | solution.py:41
  69.1 1.5 reshape.28
  70.6 4.1 %fusion.22 = f32[64,4096]{1,0:T(8,128)} fusion(bf16[512,4096]{1,0:T(8,128)(2,1)} %param.14, bf16[64,8192]{1,0:T(8,128)(2,1)S(1)} %reshape.28, s32[]{:T(128)S(6)} %select_n.8), kind=kOutput, calls=%fused_computation.24 | convolution fusion | flops 268435456 | bytes 5308420 | tf_op jit(solution)/shard_map/dot_general | solution.py:43
  74.8 0.6 dynamic-slice
  76.0 91.0 %all-reduce.8.cloned.1.call-done = f32[64,4096]{1,0:T(8,128)} async-done(((f32[64,4096]{1,0:T(8,128)}), f32[64,4096]{1,0:T(8,128)}) %all-reduce.8.cloned.1.call-update) | async-done | bytes 1048592
  167.0 1.1 multiply_reduce_fusion
  168.1 4.9 %psum.14 = f32[4]{0:T(128)S(1)} all-reduce(f32[4]{0:T(128)S(1)} %multiply_reduce_fusion), channel_id=1, replica_groups=mesh['grp'=2,'dev'=16] {'grp'}, use_global_device_ids=true, to_apply=%region_4.5 | all-reduce | flops 4 | bytes 32 | tf_op jit(solution)/shard_map/psum | solution.py:48
  173.0 1.0 fusion.24
  174.0 21.1 %all-gather.1 = bf16[16,4,4096]{2,1,0:T(4,128)(2,1)S(1)} all-gather(bf16[1,4,4096]{2,1,0:T(4,128)(2,1)S(1)} %fusion.24), channel_id=1, replica_groups=mesh['grp'=2,'dev'=16] {'dev'}, dimensions={0}, use_global_device_ids=true | all-gather | bytes 557056 | tf_op jit(solution)/shard_map/all_gather | solution.py:52
  195.1 0.1 reshape.30
  195.2 7.8 %convolution_convert_fusion = bf16[64,1792]{1,0:T(8,128)(2,1)S(1)} fusion(bf16[64,4096]{1,0:T(8,128)(2,1)S(1)} %reshape.30, bf16[4096,1792]{1,0:T(8,128)(2,1)} %param.18), kind=kOutput, calls=%fused_computation.1 | convolution fusion | flops 939638784 | bytes 15433728 | tf_op jit(solution)/shard_map/dot_general | solution.py:56
  203.0 7.8 %convolution_convert_fusion.1 = bf16[64,1792]{1,0:T(8,128)(2,1)S(1)} fusion(bf16[64,4096]{1,0:T(8,128)(2,1)S(1)} %reshape.30, bf16[4096,1792]{1,0:T(8,128)(2,1)} %param.17), kind=kOutput, calls=%fused_computation.2 | convolution fusion | flops 939638784 | bytes 15433728 | tf_op jit(solution)/shard_map/dot_general | solution.py:55
  210.8 0.8 pad_maximum_fusion
  211.7 24.5 %all-reduce.6.cloned.1.call-done = bf16[64,3584]{1,0:T(8,128)(2,1)} async-done(((bf16[64,3584]{1,0:T(8,128)(2,1)}), bf16[64,3584]{1,0:T(8,128)(2,1)}) %all-reduce.6.cloned.1.call-update) | async-done | bytes 458768 | tf_op jit(solution)/shard_map/psum | solution.py:60
  236.3 1.1 convert_element_type.34
  237.3 8.8 %fusion.17 = f32[64,4096]{1,0:T(8,128)} fusion(bf16[1792,4096]{1,0:T(8,128)(2,1)} %param.19, f32[64,3584]{1,0:T(8,128)S(1)} %convert_element_type.34), kind=kOutput, calls=%fused_computation.16 | convolution fusion | flops 940212224 | bytes 16646144 | tf_op jit(solution)/shard_map/dot_general | solution.py:66
  246.2 93.5 %all-reduce.10.cloned.1.call-done = f32[64,4096]{1,0:T(8,128)} async-done(((f32[64,4096]{1,0:T(8,128)}), f32[64,4096]{1,0:T(8,128)}) %all-reduce.10.cloned.1.call-update) | async-done | bytes 1048592
  339.7 1.6 fusion.21
  (17 shorter events, 0.2 us)
Async XLA Ops:
  6.5 1.6 copy-start
  6.5 62.6 %all-gather.4.cloned.1.call-start = ((), (), s32[]{:S(2)}) async-start(), calls=%async_computation.1 | async-start | bytes 1081344 | tf_op jit(solution)/shard_map/all_gather | solution.py:41
  12.6 154.4 %all-reduce.8.cloned.1.call-start = ((), (), s32[]{:S(2)}) async-start(), calls=%async_computation.2 | async-start | bytes 2097152
  12.6 62.1 %copy-start.3 = (u32[32]{0:T(128)S(1)}, u32[32]{0:T(128)}, u32[]{:S(2)}) copy-start(u32[32]{0:T(128)} %constant.33) | copy-start | bytes 388
  12.6 154.4 %copy-start.1 = (bf16[4,4096]{1,0:T(4,128)(2,1)S(1)}, bf16[4,4096]{1,0:T(4,128)(2,1)}, u32[]{:S(2)}) copy-start(bf16[4,4096]{1,0:T(4,128)(2,1)} %param.15) | copy-start | bytes 98308
  12.6 155.4 %copy-start.2 = (bf16[4096]{0:T(1024)(128)(2,1)S(1)}, bf16[4096]{0:T(1024)(128)(2,1)}, u32[]{:S(2)}) copy-start(bf16[4096]{0:T(1024)(128)(2,1)} %param.16) | copy-start | bytes 24580
  74.7 161.6 %all-reduce.6.cloned.1.call-start = ((), (), s32[]{:S(2)}) async-start(), calls=%async_computation | async-start | bytes 917504 | tf_op jit(solution)/shard_map/psum | solution.py:60
  211.7 128.1 %all-reduce.10.cloned.1.call-start = ((), (), s32[]{:S(2)}) async-start(), calls=%async_computation.3 | async-start | bytes 2097152
Sparse Core Ops, SparseCore 0:
  12.7 56.4 all-gather.3
  74.8 92.1 all-reduce.7
  211.8 24.4 all-reduce.5
  246.3 93.3 all-reduce.9
where the time goes:
time: 348 us
  waiting for transfers between devices  266 us (76%)
  matrix products  32.1 us (9%)
  blocking collectives  26 us (7%)
  between operations  13.9 us (4%)
  other arithmetic  6.65 us (2%)
  local copies, waits for them, and re-layouts  3.56 us (1%)
    unnamed x6, waiting for transfers between devices  185 us
    all_gather x1, waiting for transfers between devices, per_device(): lax.all_gather(attn, ('grp', 'dev'), axis=0, tiled=True)  56.5 us
    psum x1, waiting for transfers between devices, per_device(): both = lax.psum(half_terms.astype(jnp.bfloat16), 'grp').astype(jnp.float32)  24.5 us
    all_gather x1, blocking collectives, per_device(): piece = lax.all_gather(normed, 'dev', axis=0, tiled=True)  21.1 us
    dot_general x1, matrix products, per_device(): jnp.dot(hidden, down_weight, preferred_element_type=jnp.float32)  8.84 us
    dot_general x1, matrix products, per_device(): jnp.dot(piece, up_weight, preferred_element_type=jnp.float32)  7.81 us
    dot_general x1, matrix products, per_device(): jnp.dot(piece, gate_weight, preferred_element_type=jnp.float32)  7.81 us
  transfers between devices with their start and end apart: 4, of which 4 were waited for; matrix products, arithmetic and copies ran while one was open for 0% of the time, Pallas kernels for 0%

commit v1 on v0

--- a/solution.py
+++ b/solution.py
@@ -57,7 +57,9 @@
         ],
         axis=1,
     )
-    both = lax.psum(half_terms.astype(jnp.bfloat16), "grp").astype(jnp.float32)
+    both = jnp.sum(lax.all_gather(half_terms.astype(jnp.bfloat16), "grp"), axis=0).astype(
+        jnp.float32
+    )
     hidden_cols = gate_weight.shape[1]
     gate = both[:, :hidden_cols]
     up = both[:, hidden_cols:]

time: 348 us -> 333 us (0.957)
  waiting for transfers between devices: 266 us -> 238 us
  blocking collectives: 26 us -> 39.5 us
    psum x1 -> x0, waiting for transfers between devices: 24.5 us -> none  [per_device(): both = lax.psum(half_terms.astype(jnp.bfloat16), 'grp').astype(jnp.float32)]
    all_gather x0 -> x1, blocking collectives: none -> 13.4 us  [per_device(): lax.all_gather(half_terms.astype(jnp.bfloat16), 'grp')]
    unnamed x6 -> x5, waiting for transfers between devices: 185 us -> 182 us
  transfers between devices with their start and end apart: 4 -> 3, of which waited for: 4 -> 3; matrix products, arithmetic and copies ran while one was open for 0% -> 0% of each run, Pallas kernels for 0% -> 0%
where the time goes in v1:
time: 333 us; the launch traced here: 332 us
  waiting for transfers between devices  238 us (71%)
  blocking collectives  39.5 us (12%)
  matrix products  32.1 us (10%)
  between operations  13.9 us (4%)
  other arithmetic  5.19 us (2%)
  local copies, waits for them, and re-layouts  3.56 us (1%)
    unnamed x5, waiting for transfers between devices  182 us
    all_gather x1, waiting for transfers between devices, per_device(): lax.all_gather(attn, ('grp', 'dev'), axis=0, tiled=True)  56.5 us
    all_gather x1, blocking collectives, per_device(): piece = lax.all_gather(normed, 'dev', axis=0, tiled=True)  21.1 us
    all_gather x1, blocking collectives, per_device(): lax.all_gather(half_terms.astype(jnp.bfloat16), 'grp')  13.4 us
    dot_general x1, matrix products, per_device(): jnp.dot(hidden, down_weight, preferred_element_type=jnp.float32)  8.84 us
    dot_general x1, matrix products, per_device(): jnp.dot(piece, up_weight, preferred_element_type=jnp.float32)  7.81 us
    dot_general x1, matrix products, per_device(): jnp.dot(piece, gate_weight, preferred_element_type=jnp.float32)  7.81 us
  transfers between devices with their start and end apart: 3, of which 3 were waited for; matrix products, arithmetic and copies ran while one was open for 0% of the time, Pallas kernels for 0%

profile of v1, /device:TPU:0, one launch (start us, length us, event | category | flops | bytes accessed | tf_op | source)
XLA Modules:
  0.0 332.4 jit_solution(4016790907575004719)
XLA Ops:
  6.5 0.9 iota_compare_fusion
  7.4 0.7 copy-done
  8.1 1.4 fusion.12
  9.6 0.2 fusion.30
  9.8 2.1 fusion.15
  11.9 0.6 reshape.58
  12.7 56.5 %all-gather.4.cloned.1.call-done = bf16[32,2,8192]{2,1,0:T(2,128)(2,1)} async-done(((bf16[1,2,8192]{2,1,0:T(2,128)(2,1)}), bf16[32,2,8192]{2,1,0:T(2,128)(2,1)}) %all-gather.4.cloned.1.call-update) | async-done | bytes 1048592 | tf_op jit(solution)/shard_map/all_gather | solution.py:41
  69.1 1.5 reshape.59
  70.6 4.1 %fusion.24 = f32[64,4096]{1,0:T(8,128)} fusion(bf16[512,4096]{1,0:T(8,128)(2,1)} %param.14, bf16[64,8192]{1,0:T(8,128)(2,1)S(1)} %reshape.59, s32[]{:T(128)S(6)} %select_n.8), kind=kOutput, calls=%fused_computation.26 | convolution fusion | flops 268435456 | bytes 5308420 | tf_op jit(solution)/shard_map/dot_general | solution.py:43
  74.8 0.6 dynamic-slice
  76.0 91.0 %all-reduce.5.cloned.1.call-done = f32[64,4096]{1,0:T(8,128)} async-done(((f32[64,4096]{1,0:T(8,128)}), f32[64,4096]{1,0:T(8,128)}) %all-reduce.5.cloned.1.call-update) | async-done | bytes 1048592
  167.0 1.1 multiply_reduce_fusion
  168.1 4.9 %psum.7 = f32[4]{0:T(128)S(1)} all-reduce(f32[4]{0:T(128)S(1)} %multiply_reduce_fusion), channel_id=1, replica_groups=mesh['grp'=2,'dev'=16] {'grp'}, use_global_device_ids=true, to_apply=%region_4.5 | all-reduce | flops 4 | bytes 32 | tf_op jit(solution)/shard_map/psum | solution.py:48
  173.0 1.0 fusion.26
  174.0 21.1 %all-gather.1 = bf16[16,4,4096]{2,1,0:T(4,128)(2,1)S(1)} all-gather(bf16[1,4,4096]{2,1,0:T(4,128)(2,1)S(1)} %fusion.26), channel_id=1, replica_groups=mesh['grp'=2,'dev'=16] {'dev'}, dimensions={0}, use_global_device_ids=true | all-gather | bytes 557056 | tf_op jit(solution)/shard_map/all_gather | solution.py:52
  195.1 0.1 reshape.61
  195.2 7.8 %fusion.2 = bf16[1,64,1792]{2,1,0:T(8,128)(2,1)S(1)} fusion(bf16[64,4096]{1,0:T(8,128)(2,1)S(1)} %reshape.61, bf16[4096,1792]{1,0:T(8,128)(2,1)} %param.18), kind=kOutput, calls=%fused_computation.4 | convolution fusion | flops 939638784 | bytes 15433728 | tf_op jit(solution)/shard_map/dot_general | solution.py:56
  203.0 7.8 %fusion.1 = bf16[1,64,1792]{2,1,0:T(8,128)(2,1)S(1)} fusion(bf16[64,4096]{1,0:T(8,128)(2,1)S(1)} %reshape.61, bf16[4096,1792]{1,0:T(8,128)(2,1)} %param.17), kind=kOutput, calls=%fused_computation.3 | convolution fusion | flops 939638784 | bytes 15433728 | tf_op jit(solution)/shard_map/dot_general | solution.py:55
  210.9 13.4 %all_gather.12 = bf16[2,64,3584]{2,1,0:T(8,128)(2,1)S(1)} all-gather(bf16[1,64,3584]{2,1,0:T(8,128)(2,1)S(1)} %pad_maximum_fusion), channel_id=1, replica_groups=mesh['grp'=2,'dev'=16] {'grp'}, dimensions={0}, use_global_device_ids=true | all-gather | bytes 1376256 | tf_op jit(solution)/shard_map/all_gather | solution.py:60
  224.3 0.3 reduce_sum.32
  224.7 0.1 convert_element_type.43
  224.7 8.8 %fusion.19 = f32[64,4096]{1,0:T(8,128)} fusion(bf16[1792,4096]{1,0:T(8,128)(2,1)} %param.19, f32[64,3584]{1,0:T(8,128)S(1)} %convert_element_type.43), kind=kOutput, calls=%fused_computation.18 | convolution fusion | flops 940212224 | bytes 16646144 | tf_op jit(solution)/shard_map/dot_general | solution.py:68
  233.6 90.6 %all-reduce.7.cloned.1.call-done = f32[64,4096]{1,0:T(8,128)} async-done(((f32[64,4096]{1,0:T(8,128)}), f32[64,4096]{1,0:T(8,128)}) %all-reduce.7.cloned.1.call-update) | async-done | bytes 1048592
  324.2 1.6 fusion.23
  (16 shorter events, 0.2 us)
Async XLA Ops:
  6.5 1.6 copy-start
  6.5 62.6 %all-gather.4.cloned.1.call-start = ((), (), s32[]{:S(2)}) async-start(), calls=%async_computation | async-start | bytes 1081344 | tf_op jit(solution)/shard_map/all_gather | solution.py:41
  12.6 154.4 %all-reduce.5.cloned.1.call-start = ((), (), s32[]{:S(2)}) async-start(), calls=%async_computation.1 | async-start | bytes 2097152
  12.6 62.1 %copy-start.3 = (u32[32]{0:T(128)S(1)}, u32[32]{0:T(128)}, u32[]{:S(2)}) copy-start(u32[32]{0:T(128)} %constant.35) | copy-start | bytes 388
  12.6 154.4 %copy-start.1 = (bf16[4,4096]{1,0:T(4,128)(2,1)S(1)}, bf16[4,4096]{1,0:T(4,128)(2,1)}, u32[]{:S(2)}) copy-start(bf16[4,4096]{1,0:T(4,128)(2,1)} %param.15) | copy-start | bytes 98308
  12.6 155.4 %copy-start.2 = (bf16[4096]{0:T(1024)(128)(2,1)S(1)}, bf16[4096]{0:T(1024)(128)(2,1)}, u32[]{:S(2)}) copy-start(bf16[4096]{0:T(1024)(128)(2,1)} %param.16) | copy-start | bytes 24580
  74.7 249.5 %all-reduce.7.cloned.1.call-start = ((), (), s32[]{:S(2)}) async-start(), calls=%async_computation.2 | async-start | bytes 2097152
Sparse Core Ops, SparseCore 0:
  12.7 56.4 all-gather.3
  74.8 92.1 all-reduce.4
  233.7 90.4 all-reduce.6
